TPU v7x, 256 devices: a whole 4x4x8 slice. The times are simulated.
256 devices in a mesh: fsdp: 16 (over x, z_lo, core), replica: 16 (over y, z_hi).
Axes of the slice: x: 4, y: 4, z: 8 (z_hi: 4, z_lo: 2; z = z_hi * 2 + z_lo), core: 2. Of those that a mesh axis runs over, the one named last changes fastest.
Arguments:
- weights: float32 [256, 512, 2048], P('replica', 'fsdp'), may hold values from -0.125 to 0.125
- momentum: bfloat16 [256, 512, 2048], P('replica', 'fsdp'), may hold values from -6 to 6
- tokens: bfloat16 [229376, 2048], P(('fsdp', 'replica')), may hold values from -6 to 6
- block_expert: int32 [1792], P(('fsdp', 'replica')), may hold values from 0 to 255, as said below
- owner_expert: int32 [256], replicated, may hold values from 0 to 255, as said below
Outputs:
- fresh: bfloat16 [256, 512, 2048], P(('fsdp', 'replica'))
- rollout: bfloat16 [229376, 512], P(('fsdp', 'replica'))
Inputs may be any that keep to these rules, and one draw needn't show every extreme that they name: `owner_expert`: within each group g the entries g * N to g * N + N - 1 (N the fsdp axis size) are a permutation of the expert numbers g * N to g * N + N - 1. `block_expert`: the blocks of the device at fsdp index f and replica index r are blocks (f * R + r) * 7 to (f * R + r) * 7 + 7 - 1 (R the replica axis size). Each names an expert that owner_expert assigns to fsdp index f; the 7 blocks of one device name experts of distinct groups; in every fsdp index one group is named by every device of that index.
All inputs are finite; a program needn't handle non-finite values.
Results may differ from a plain program's by a relative error of at most 0.008.
Values may be sent and summed in bfloat16 or wider, within the bound.
A program may use at most 128 MiB of HBM per device.

v0:
```python
import math
import jax
import jax.numpy as jnp
from jax import lax
from jax.sharding import PartitionSpec as P

ROWS_E = 512
COLS = 2048
ITERS = 4
quintic_one = 3.4445
quintic_two = -4.775
quintic_three = 2.0315
learn_rate = 0.05
weight_decay = 0.1
norm_eps = 1e-07


def orthogonalize(moment):
    wide = moment.astype(jnp.float32)
    state = (wide / (jnp.sqrt(jnp.sum(wide * wide)) + norm_eps)).astype(jnp.bfloat16)
    for _ in range(ITERS):
        square = lax.dot_general(
            state, state, (((1,), (1,)), ((), ())), preferred_element_type=jnp.float32
        ).astype(jnp.bfloat16)
        twice = jnp.dot(square, square, preferred_element_type=jnp.float32)
        poly = (quintic_two * square.astype(jnp.float32) + quintic_three * twice).astype(
            jnp.bfloat16
        )
        state = (
            quintic_one * state.astype(jnp.float32)
            + jnp.dot(poly, state, preferred_element_type=jnp.float32)
        ).astype(jnp.bfloat16)
    return state


def finish(master, update):
    factor = learn_rate * 0.2 * math.sqrt(max(ROWS_E, COLS))
    return (
        master * (1.0 - learn_rate * weight_decay) - factor * update.astype(jnp.float32)
    ).astype(jnp.bfloat16)


def per_device(weights, momentum, tokens, block_expert, owner_expert):
    owners = lax.axis_size("fsdp")
    groups = lax.axis_size("replica")
    group = lax.axis_index("replica")
    table = lax.dynamic_slice_in_dim(owner_expert, group * owners, owners, 0)
    local = table - group * owners
    sent_moment = jnp.take(momentum, local, axis=0)
    sent_master = jnp.take(weights, local, axis=0)
    whole_master, whole_moment = (
        lax.all_to_all(sent_master, "fsdp", split_axis=0, concat_axis=1, tiled=True),
        lax.all_to_all(
            sent_moment.astype(jnp.float32), "fsdp", split_axis=0, concat_axis=1, tiled=True
        ),
    )
    update = orthogonalize(whole_moment[0].astype(jnp.bfloat16))
    refreshed = finish(whole_master[0], update)
    fresh = refreshed[None]
    blocks = block_expert.shape[0]
    width = tokens.shape[1]
    resident = tokens.reshape(blocks, -1, width)
    target = block_expert // owners
    selector = (target[:, None] == jnp.arange(groups, dtype=jnp.int32)[None, :]).astype(
        jnp.bfloat16
    )
    outgoing = jnp.einsum(
        "bg,brd->grd", selector, resident, preferred_element_type=jnp.float32
    ).astype(jnp.bfloat16)
    product = jnp.einsum(
        "grd,od->gro",
        lax.all_to_all(outgoing, "replica", split_axis=0, concat_axis=0, tiled=True),
        refreshed,
        preferred_element_type=jnp.float32,
    ).astype(jnp.bfloat16)
    answers = lax.all_to_all(product, "replica", split_axis=0, concat_axis=0, tiled=True)
    picked = jnp.einsum(
        "bg,gro->bro", selector, answers, preferred_element_type=jnp.float32
    ).astype(jnp.bfloat16)
    rollout = picked.reshape(-1, answers.shape[2])
    return (fresh, rollout)


def solution(mesh):
    placed = (
        P("replica", "fsdp", None),
        P("replica", "fsdp", None),
        P(("fsdp", "replica"), None),
        P(("fsdp", "replica")),
        P(),
    )
    return jax.shard_map(
        per_device,
        mesh=mesh,
        in_specs=placed,
        out_specs=(P(("fsdp", "replica"), None, None), P(("fsdp", "replica"), None)),
        check_vma=False,
    )
```

profile of v0, /device:TPU:6, one launch (start us, length us, event | category | flops | bytes accessed | tf_op | source)
XLA Modules:
  0.0 393.0 jit_solution(13910733482584841381)
XLA Ops:
  2.2 2.0 gather_fusion.1
  4.2 3.2 select_convert_fusion
  7.4 6.1 %all-to-all-start.1 = ((bf16[16,32,2048]{2,1,0:T(8,128)(2,1)}), bf16[16,32,2048]{2,1,0:T(8,128)(2,1)S(1)}, u32[]{:S(2)}, u32[]{:S(2)}) async-start(bf16[16,32,2048]{2,1,0:T(8,128)(2,1)} %select_convert_fusion), calls=%async_computation.1 | async-start | bytes 4194304 | tf_op jit(solution)/shard_map/all_to_all | solution.py:53
  13.6 5.0 %gather_fusion = f32[16,32,2048]{2,1,0:T(8,128)} fusion(f32[16,32,2048]{2,1,0:T(8,128)} %param.5, s32[1024]{0:T(1024)S(1)} %pad_clamp_fusion), kind=kCustom, calls=%fused_computation | custom fusion | bytes 8388672 | tf_op jit(solution)/shard_map/jit(_take)/gather | solution.py:50
  18.5 4.9 %broadcast_select_fusion = f32[16,32,2048]{2,1,0:T(8,128)} fusion(f32[16,32,2048]{2,1,0:T(8,128)} %gather_fusion, pred[16]{0:T(512)(128)(4,1)S(1)} %get-tuple-element.2), kind=kLoop, calls=%fused_computation.21 | loop fusion | flops 1048576 | bytes 8388624 | tf_op jit(solution)/shard_map/jit(_take)/select_n | solution.py:50
  23.4 16.3 %all-to-all-done.1 = bf16[16,32,2048]{2,1,0:T(8,128)(2,1)S(1)} async-done(((bf16[16,32,2048]{2,1,0:T(8,128)(2,1)}), bf16[16,32,2048]{2,1,0:T(8,128)(2,1)S(1)}, u32[]{:S(2)}, u32[]{:S(2)}) %all-to-all-start.1) | async-done | bytes 2097184 | tf_op jit(solution)/shard_map/all_to_all | solution.py:53
  39.8 6.1 %all-to-all-start = ((f32[16,32,2048]{2,1,0:T(8,128)}), f32[16,32,2048]{2,1,0:T(8,128)}, u32[]{:S(2)}, u32[]{:S(2)}) async-start(f32[16,32,2048]{2,1,0:T(8,128)} %broadcast_select_fusion), calls=%async_computation | async-start | bytes 8388608 | tf_op jit(solution)/shard_map/all_to_all | solution.py:52
  45.8 8.3 %convolution_convert_fusion = bf16[16,128,2048]{2,0,1:T(8,128)(2,1)} fusion(bf16[7,128,2048]{2,1,0:T(8,128)(2,1)} %bitcast.37, s32[7]{0:T(128)S(1)} %and_select_fusion), kind=kOutput, calls=%fused_computation.4 | convolution fusion | flops 62914672 | bytes 12058652 | tf_op jit(solution)/shard_map/bg,brd->grd/dot_general | solution.py:67
  54.1 11.2 %copy.13 = bf16[16,128,2048]{2,1,0:T(8,128)(2,1)} copy(bf16[16,128,2048]{2,0,1:T(8,128)(2,1)} %convolution_convert_fusion) | data formatting | bytes 16777216 | tf_op jit(solution)/shard_map/convert_element_type | solution.py:69
  65.4 29.2 %all-to-all-done = f32[16,32,2048]{2,1,0:T(8,128)} async-done(((f32[16,32,2048]{2,1,0:T(8,128)}), f32[16,32,2048]{2,1,0:T(8,128)}, u32[]{:S(2)}, u32[]{:S(2)}) %all-to-all-start) | async-done | bytes 4194336 | tf_op jit(solution)/shard_map/all_to_all | solution.py:52
  94.6 10.4 %all-to-all-start.2 = ((bf16[16,128,2048]{2,1,0:T(8,128)(2,1)}), bf16[16,128,2048]{2,1,0:T(8,128)(2,1)}, u32[]{:S(2)}, u32[]{:S(2)}) async-start(bf16[16,128,2048]{2,1,0:T(8,128)(2,1)} %copy.13), calls=%async_computation.2 | async-start | bytes 16777216 | tf_op jit(solution)/shard_map/all_to_all | solution.py:72
  105.0 1.7 fusion.2
  107.8 1.3 copy-done.2
  110.4 3.8 add_convert_fusion.3
  114.2 1.3 convolution_convert_fusion.3
  115.5 2.9 add_convert_fusion.2
  118.3 3.5 convolution_convert_fusion.2
  121.8 3.8 add_convert_fusion.1
  125.6 1.3 convolution_convert_fusion.1
  126.9 4.9 %broadcast_multiply_fusion = f32[16,32,2048]{2,1,0:T(8,128)} fusion(f32[16,32,2048]{2,1,0:T(8,128)} %all-to-all-done), kind=kLoop, calls=%fused_computation.20 | loop fusion | flops 1048576 | bytes 8388608 | tf_op jit(solution)/shard_map/mul | solution.py:39
  131.8 4.7 %fusion.4 = bf16[512,2048]{1,0:T(8,128)(2,1)} fusion(f32[16,32,2048]{2,1,0:T(8,128)} %broadcast_multiply_fusion, bf16[512,2048]{1,0:T(8,128)(2,1)S(1)} %add_convert_fusion.1, bf16[512,512]{1,0:T(8,128)(2,1)S(1)} %convolution_convert_fusion.1), kind=kOutput, calls=%fused_computation.10 | convolution fusion | flops 1351876608 | bytes 8912896 | tf_op jit(solution)/shard_map/dot_general | solution.py:31
  136.5 191.0 %all-to-all-done.2 = bf16[16,128,2048]{2,1,0:T(8,128)(2,1)} async-done(((bf16[16,128,2048]{2,1,0:T(8,128)(2,1)}), bf16[16,128,2048]{2,1,0:T(8,128)(2,1)}, u32[]{:S(2)}, u32[]{:S(2)}) %all-to-all-start.2) | async-done | bytes 8388640 | tf_op jit(solution)/shard_map/all_to_all | solution.py:72
  327.5 10.9 %fusion.9 = bf16[16,128,512]{2,0,1:T(8,128)(2,1)S(1)} fusion(bf16[512,2048]{1,0:T(8,128)(2,1)} %fusion.4, bf16[16,128,2048]{2,1,0:T(8,128)(2,1)} %all-to-all-done.2), kind=kOutput, calls=%fused_computation.22 | convolution fusion | flops 4296015872 | bytes 12582912 | tf_op jit(solution)/shard_map/grd,od->gro/dot_general | solution.py:70
  339.6 50.9 %all_to_all.28 = bf16[16,128,512]{2,1,0:T(8,128)(2,1)S(1)} all-to-all(bf16[16,128,512]{2,1,0:T(8,128)(2,1)S(1)} %copy.15), channel_id=1, replica_groups=mesh['fsdp'=16,'replica'=16] {'replica'}, dimensions={0} | all-to-all | bytes 4194304 | tf_op jit(solution)/shard_map/all_to_all | solution.py:76
  (15 shorter events, 7.0 us)
Async XLA Ops:
  0.6 1.6 copy-start
  7.4 32.3 %all-to-all-start.1 = ((bf16[16,32,2048]{2,1,0:T(8,128)(2,1)}), bf16[16,32,2048]{2,1,0:T(8,128)(2,1)S(1)}, u32[]{:S(2)}, u32[]{:S(2)}) async-start(bf16[16,32,2048]{2,1,0:T(8,128)(2,1)} %select_convert_fusion), calls=%async_computation.1 | async-start | bytes 4194304 | tf_op jit(solution)/shard_map/all_to_all | solution.py:53
  23.4 22.4 %copy-start.3 = (s32[7]{0:T(128)S(1)}, s32[7]{0:T(128)}, u32[]{:S(2)}) copy-start(s32[7]{0:T(128)} %param.8) | copy-start | bytes 88
  39.8 54.8 %all-to-all-start = ((f32[16,32,2048]{2,1,0:T(8,128)}), f32[16,32,2048]{2,1,0:T(8,128)}, u32[]{:S(2)}, u32[]{:S(2)}) async-start(f32[16,32,2048]{2,1,0:T(8,128)} %broadcast_select_fusion), calls=%async_computation | async-start | bytes 8388608 | tf_op jit(solution)/shard_map/all_to_all | solution.py:52
  94.6 232.9 %all-to-all-start.2 = ((bf16[16,128,2048]{2,1,0:T(8,128)(2,1)}), bf16[16,128,2048]{2,1,0:T(8,128)(2,1)}, u32[]{:S(2)}, u32[]{:S(2)}) async-start(bf16[16,128,2048]{2,1,0:T(8,128)(2,1)} %copy.13), calls=%async_computation.2 | async-start | bytes 16777216 | tf_op jit(solution)/shard_map/all_to_all | solution.py:72
  107.8 1.3 copy-start.2
  339.6 53.4 %copy-start.1 = (bf16[16,32,2048]{2,1,0:T(8,128)(2,1)S(1)}, bf16[16,32,2048]{2,1,0:T(8,128)(2,1)}, u32[]{:S(2)}) copy-start(bf16[16,32,2048]{2,1,0:T(8,128)(2,1)} %param.6) | copy-start | bytes 6291460
where the time goes:
time: 394 us; the launch traced here: 393 us
  waiting for transfers between devices  237 us (60%)
  blocking collectives  50.9 us (13%)
  matrix products  42.9 us (11%)
  local copies, waits for them, and re-layouts  22.6 us (6%)
  starting transfers between devices  22.6 us (6%)
  other arithmetic  16 us (4%)
    all_to_all x1, waiting for transfers between devices, per_device(): lax.all_to_all(outgoing, 'replica', split_axis=0, concat_axis=0, tiled=True)  191 us
    all_to_all x1, blocking collectives, per_device(): lax.all_to_all(product, 'replica', split_axis=0, concat_axis=0, tiled=True)  50.9 us
    all_to_all x1, waiting for transfers between devices, per_device(): lax.all_to_all(sent_master, 'fsdp', split_axis=0, concat_axis=1, tiled=True)  29.2 us
    all_to_all x1, waiting for transfers between devices, per_device(): lax.all_to_all(sent_moment.astype(jnp.float32), 'fsdp', split_axis=0, con...  16.3 us
    dot_general x4, matrix products, orthogonalize(): jnp.dot(poly, state, preferred_element_type=jnp.float32)  15.2 us
    convert_element_type x1, local copies, waits for them, and re-layouts, per_device(): outgoing = jnp.einsum('bg,brd->grd', selector, resident, preferred_elemen...  11.2 us
    dot_general x1, matrix products, per_device(): jnp.einsum('grd,od->gro', lax.all_to_all(outgoing, 'replica', split_axis=...  10.9 us
    all_to_all x1, starting transfers between devices, per_device(): lax.all_to_all(outgoing, 'replica', split_axis=0, concat_axis=0, tiled=True)  10.4 us
  transfers between devices with their start and end apart: 3, of which 3 were waited for; matrix products, arithmetic and copies ran while one was open for 15% of the time, Pallas kernels for 0%

commit v1 on v0

--- a/solution.py
+++ b/solution.py
@@ -13,6 +13,15 @@
 learn_rate = 0.05
 weight_decay = 0.1
 norm_eps = 1e-07
+
+
+def _cut_sources_all(arr, axis_key="fsdp"):
+    return jnp.concatenate(
+        lax.all_to_all(
+            jnp.stack(jnp.split(arr, lax.axis_size(axis_key), axis=0), axis=0), axis_key, 0, 0
+        ),
+        axis=1,
+    )
 
 
 def orthogonalize(moment):
@@ -50,9 +59,7 @@
     sent_master = jnp.take(weights, local, axis=0)
     whole_master, whole_moment = (
         lax.all_to_all(sent_master, "fsdp", split_axis=0, concat_axis=1, tiled=True),
-        lax.all_to_all(
-            sent_moment.astype(jnp.float32), "fsdp", split_axis=0, concat_axis=1, tiled=True
-        ),
+        _cut_sources_all(sent_moment.astype(jnp.float32)),
     )
     update = orthogonalize(whole_moment[0].astype(jnp.bfloat16))
     refreshed = finish(whole_master[0], update)

time: 394 us -> 403 us (1.023)
  local copies, waits for them, and re-layouts: 22.6 us -> 33.3 us
    unnamed x8 -> x23, local copies, waits for them, and re-layouts: 2.01 us -> 12 us
where the time goes in v1:
time: 403 us; the launch traced here: 402 us
  waiting for transfers between devices  237 us (59%)
  blocking collectives  50.9 us (13%)
  matrix products  42.9 us (11%)
  local copies, waits for them, and re-layouts  33.3 us (8%)
  starting transfers between devices  22.6 us (6%)
  other arithmetic  14.7 us (4%)
    all_to_all x1, waiting for transfers between devices, per_device(): lax.all_to_all(outgoing, 'replica', split_axis=0, concat_axis=0, tiled=True)  191 us
    all_to_all x1, blocking collectives, per_device(): lax.all_to_all(product, 'replica', split_axis=0, concat_axis=0, tiled=True)  50.9 us
    all_to_all x1, waiting for transfers between devices, per_device(): lax.all_to_all(sent_master, 'fsdp', split_axis=0, concat_axis=1, tiled=True)  29.2 us
    all_to_all x1, waiting for transfers between devices, _cut_sources_all(): lax.all_to_all(jnp.stack(jnp.split(arr, lax.axis_size(axis_key), axis=0),...  16.3 us
    dot_general x4, matrix products, orthogonalize(): jnp.dot(poly, state, preferred_element_type=jnp.float32)  15.2 us
    unnamed x23, local copies, waits for them, and re-layouts  12 us
    convert_element_type x1, local copies, waits for them, and re-layouts, per_device(): outgoing = jnp.einsum('bg,brd->grd', selector, resident, preferred_elemen...  11.2 us
    dot_general x1, matrix products, per_device(): jnp.einsum('grd,od->gro', lax.all_to_all(outgoing, 'replica', split_axis=...  10.8 us
  transfers between devices with their start and end apart: 3, of which 3 were waited for; matrix products, arithmetic and copies ran while one was open for 15% of the time, Pallas kernels for 0%

profile of v1, /device:TPU:6, one launch (start us, length us, event | category | flops | bytes accessed | tf_op | source)
XLA Modules:
  0.0 402.3 jit_solution(3207295077350428344)
XLA Ops:
  2.2 2.0 gather_fusion.1
  4.2 1.9 select_convert_fusion
  16.7 6.1 %all-to-all-start.1 = ((bf16[16,1,32,2048]{3,2,1,0:T(8,128)(2,1)}), bf16[16,1,32,2048]{3,2,1,0:T(8,128)(2,1)S(1)}, u32[]{:S(2)}, u32[]{:S(2)}) async-start(bf16[16,1,32,2048]{3,2,1,0:T(8,128)(2,1)} %fusion.33), calls=%async_computation.1 | async-start | bytes 4194304 | tf_op jit(solution)/shard_map/all_to_all | solution.py:20
  22.9 5.0 %gather_fusion = f32[16,32,2048]{2,1,0:T(8,128)} fusion(f32[16,32,2048]{2,1,0:T(8,128)} %param.5, s32[1024]{0:T(1024)S(1)} %pad_clamp_fusion), kind=kCustom, calls=%fused_computation | custom fusion | bytes 8388672 | tf_op jit(solution)/shard_map/jit(_take)/gather | solution.py:59
  27.9 4.9 %broadcast_select_fusion = f32[16,32,2048]{2,1,0:T(8,128)} fusion(f32[16,32,2048]{2,1,0:T(8,128)} %gather_fusion, pred[16]{0:T(512)(128)(4,1)S(1)} %get-tuple-element.2), kind=kLoop, calls=%fused_computation.21 | loop fusion | flops 1048576 | bytes 8388624 | tf_op jit(solution)/shard_map/jit(_take)/select_n | solution.py:59
  32.7 16.3 %all-to-all-done.1 = bf16[16,1,32,2048]{3,2,1,0:T(8,128)(2,1)S(1)} async-done(((bf16[16,1,32,2048]{3,2,1,0:T(8,128)(2,1)}), bf16[16,1,32,2048]{3,2,1,0:T(8,128)(2,1)S(1)}, u32[]{:S(2)}, u32[]{:S(2)}) %all-to-all-start.1) | async-done | bytes 2097184 | tf_op jit(solution)/shard_map/all_to_all | solution.py:20
  49.1 6.1 %all-to-all-start = ((f32[16,32,2048]{2,1,0:T(8,128)}), f32[16,32,2048]{2,1,0:T(8,128)}, u32[]{:S(2)}, u32[]{:S(2)}) async-start(f32[16,32,2048]{2,1,0:T(8,128)} %broadcast_select_fusion), calls=%async_computation | async-start | bytes 8388608 | tf_op jit(solution)/shard_map/all_to_all | solution.py:61
  55.1 8.3 %convolution_convert_fusion = bf16[16,128,2048]{2,0,1:T(8,128)(2,1)} fusion(bf16[7,128,2048]{2,1,0:T(8,128)(2,1)} %bitcast.101, s32[7]{0:T(128)S(1)} %and_select_fusion), kind=kOutput, calls=%fused_computation.4 | convolution fusion | flops 62914672 | bytes 12058652 | tf_op jit(solution)/shard_map/bg,brd->grd/dot_general | solution.py:74
  63.5 11.2 %copy.13 = bf16[16,128,2048]{2,1,0:T(8,128)(2,1)} copy(bf16[16,128,2048]{2,0,1:T(8,128)(2,1)} %convolution_convert_fusion) | data formatting | bytes 16777216 | tf_op jit(solution)/shard_map/convert_element_type | solution.py:76
  74.7 29.2 %all-to-all-done = f32[16,32,2048]{2,1,0:T(8,128)} async-done(((f32[16,32,2048]{2,1,0:T(8,128)}), f32[16,32,2048]{2,1,0:T(8,128)}, u32[]{:S(2)}, u32[]{:S(2)}) %all-to-all-start) | async-done | bytes 4194336 | tf_op jit(solution)/shard_map/all_to_all | solution.py:61
  103.9 10.4 %all-to-all-start.2 = ((bf16[16,128,2048]{2,1,0:T(8,128)(2,1)}), bf16[16,128,2048]{2,1,0:T(8,128)(2,1)}, u32[]{:S(2)}, u32[]{:S(2)}) async-start(bf16[16,128,2048]{2,1,0:T(8,128)(2,1)} %copy.13), calls=%async_computation.2 | async-start | bytes 16777216 | tf_op jit(solution)/shard_map/all_to_all | solution.py:79
  114.3 1.7 fusion.2
  117.1 1.3 copy-done.2
  119.7 3.8 add_convert_fusion.3
  123.5 1.3 convolution_convert_fusion.3
  124.8 2.9 add_convert_fusion.2
  127.7 3.5 convolution_convert_fusion.2
  131.2 3.8 add_convert_fusion.1
  135.0 1.3 convolution_convert_fusion.1
  136.2 4.9 %broadcast_multiply_fusion = f32[16,32,2048]{2,1,0:T(8,128)} fusion(f32[16,32,2048]{2,1,0:T(8,128)} %all-to-all-done), kind=kLoop, calls=%fused_computation.20 | loop fusion | flops 1048576 | bytes 8388608 | tf_op jit(solution)/shard_map/mul | solution.py:48
  141.2 4.7 %fusion.4 = bf16[512,2048]{1,0:T(8,128)(2,1)} fusion(f32[16,32,2048]{2,1,0:T(8,128)} %broadcast_multiply_fusion, bf16[512,2048]{1,0:T(8,128)(2,1)S(1)} %add_convert_fusion.1, bf16[512,512]{1,0:T(8,128)(2,1)S(1)} %convolution_convert_fusion.1), kind=kOutput, calls=%fused_computation.10 | convolution fusion | flops 1351876608 | bytes 8912896 | tf_op jit(solution)/shard_map/dot_general | solution.py:40
  145.9 191.0 %all-to-all-done.2 = bf16[16,128,2048]{2,1,0:T(8,128)(2,1)} async-done(((bf16[16,128,2048]{2,1,0:T(8,128)(2,1)}), bf16[16,128,2048]{2,1,0:T(8,128)(2,1)}, u32[]{:S(2)}, u32[]{:S(2)}) %all-to-all-start.2) | async-done | bytes 8388640 | tf_op jit(solution)/shard_map/all_to_all | solution.py:79
  336.9 10.8 %fusion.9 = bf16[16,128,512]{2,0,1:T(8,128)(2,1)S(1)} fusion(bf16[512,2048]{1,0:T(8,128)(2,1)} %fusion.4, bf16[16,128,2048]{2,1,0:T(8,128)(2,1)} %all-to-all-done.2), kind=kOutput, calls=%fused_computation.22 | convolution fusion | flops 4296015872 | bytes 12582912 | tf_op jit(solution)/shard_map/grd,od->gro/dot_general | solution.py:77
  348.9 50.9 %all_to_all.24 = bf16[16,128,512]{2,1,0:T(8,128)(2,1)S(1)} all-to-all(bf16[16,128,512]{2,1,0:T(8,128)(2,1)S(1)} %copy.15), channel_id=1, replica_groups=mesh['fsdp'=16,'replica'=16] {'replica'}, dimensions={0} | all-to-all | bytes 4194304 | tf_op jit(solution)/shard_map/all_to_all | solution.py:83
  (31 shorter events, 17.6 us)
Async XLA Ops:
  0.6 1.6 copy-start
  16.7 32.3 %all-to-all-start.1 = ((bf16[16,1,32,2048]{3,2,1,0:T(8,128)(2,1)}), bf16[16,1,32,2048]{3,2,1,0:T(8,128)(2,1)S(1)}, u32[]{:S(2)}, u32[]{:S(2)}) async-start(bf16[16,1,32,2048]{3,2,1,0:T(8,128)(2,1)} %fusion.33), calls=%async_computation.1 | async-start | bytes 4194304 | tf_op jit(solution)/shard_map/all_to_all | solution.py:20
  32.7 22.4 %copy-start.3 = (s32[7]{0:T(128)S(1)}, s32[7]{0:T(128)}, u32[]{:S(2)}) copy-start(s32[7]{0:T(128)} %param.8) | copy-start | bytes 88
  49.1 54.8 %all-to-all-start = ((f32[16,32,2048]{2,1,0:T(8,128)}), f32[16,32,2048]{2,1,0:T(8,128)}, u32[]{:S(2)}, u32[]{:S(2)}) async-start(f32[16,32,2048]{2,1,0:T(8,128)} %broadcast_select_fusion), calls=%async_computation | async-start | bytes 8388608 | tf_op jit(solution)/shard_map/all_to_all | solution.py:61
  103.9 232.9 %all-to-all-start.2 = ((bf16[16,128,2048]{2,1,0:T(8,128)(2,1)}), bf16[16,128,2048]{2,1,0:T(8,128)(2,1)}, u32[]{:S(2)}, u32[]{:S(2)}) async-start(bf16[16,128,2048]{2,1,0:T(8,128)(2,1)} %copy.13), calls=%async_computation.2 | async-start | bytes 16777216 | tf_op jit(solution)/shard_map/all_to_all | solution.py:79
  117.1 1.3 copy-start.2
  348.9 53.4 %copy-start.1 = (bf16[16,32,2048]{2,1,0:T(8,128)(2,1)S(1)}, bf16[16,32,2048]{2,1,0:T(8,128)(2,1)}, u32[]{:S(2)}) copy-start(bf16[16,32,2048]{2,1,0:T(8,128)(2,1)} %param.6) | copy-start | bytes 6291460
